TPU v7x, 256 devices: a whole 4x4x8 slice. The times are simulated.
256 devices in a mesh: store: 32 (over y, z), tp: 8 (over x, core).
Axes of the slice: x: 4, y: 4, z: 8, core: 2. Of those that a mesh axis runs over, the one named last changes fastest.
Arguments:
- queries: bfloat16 [32768, 8192], P('store', 'tp')
- fresh_kv: bfloat16 [2, 32768, 1024], P(None, ('store', 'tp'))
- page_pool: bfloat16 [2048, 2, 128, 1024], P('store', None, None, 'tp')
- page_host: int32 [128, 8], P('store'), may hold values from 0 to 31, as said below
- page_slot: int32 [128, 8], P('store'), may hold values from 0 to 63, as said below
- prefix_len: int32 [128], P('store'), may hold values from 513 to 1024
- fresh_len: int32 [32, 4], P('store'), may hold values from 1 to 384, 1024 in all within a row
Outputs:
- attention: bfloat16 [32768, 8192], P('store', 'tp')
Inputs may be any that keep to these rules, and one draw needn't show every extreme that they name: `page_host`: page p of request r is read only if p < ceil(prefix_len[r] / 128). Among the pages read by the 4 requests of one host, at most 2 lie on any one host; in every draw some host holds exactly 2 of the pages read by each host. `page_slot`: several entries may name the same stored page. `fresh_len`: the requests of a host own consecutive rows of its block, in order.
All inputs are finite; a program needn't handle non-finite values.
Results may differ from a plain program's by a relative error of at most 0.0041.
Values may be sent and summed in bfloat16 or wider, within the bound.
A program may use at most 128 MiB of HBM per device.

v0:
```python
import math
import jax
import jax.numpy as jnp
from jax import lax
from jax.sharding import PartitionSpec as P

HD = 128
REQ_HOST = 4
PAGE = 128
PAGES_MAX = 8
MOST_NEW = 384


def plan_requests(owners, slot_ids, prefix, stores, capacity):
    entry_count = owners.shape[0] * owners.shape[1]
    page_count = (prefix + PAGE - 1) // PAGE
    in_use = (jnp.arange(owners.shape[1], dtype=jnp.int32)[None, :] < page_count[:, None]).reshape(
        entry_count
    )
    flat_owners = owners.reshape(entry_count)
    flat_slots = slot_ids.reshape(entry_count)
    entries = jnp.arange(entry_count, dtype=jnp.int32)
    same_owner = (
        (flat_owners[:, None] == flat_owners[None, :])
        & in_use[None, :]
        & (entries[None, :] < entries[:, None])
    )
    owner_rank = jnp.sum(same_owner.astype(jnp.int32), axis=1)
    position = jnp.where(in_use, flat_owners * capacity + owner_rank, 0)
    target = jnp.arange(stores * capacity, dtype=jnp.int32)
    matches = (position[:, None] == target[None, :]) & in_use[:, None]
    buffer = jnp.sum(jnp.where(matches, flat_slots[:, None], 0), axis=0)
    return (buffer.reshape(stores, capacity), position)


def attend(q_rows, key_rows, value_rows, key_valid):
    scores = jnp.einsum("mkgd,nkd->kgmn", q_rows, key_rows, preferred_element_type=jnp.float32) * (
        1.0 / math.sqrt(HD)
    )
    row_top = jnp.max(jnp.where(key_valid, scores, -1e30), axis=-1, keepdims=True)
    weights = jnp.where(key_valid, jnp.exp(scores - row_top), 0.0)
    row_total = jnp.sum(weights, axis=-1)
    rounded = weights.astype(jnp.bfloat16)
    mixed_rows = jnp.einsum(
        "kgmn,nkd->mkgd", rounded, value_rows, preferred_element_type=jnp.float32
    )
    return (mixed_rows / jnp.transpose(row_total, (2, 0, 1))[..., None]).astype(jnp.bfloat16)


def local(queries, fresh_kv, page_pool, page_host, page_slot, prefix_len, fresh_len):
    stores = lax.axis_size("store")
    block_rows = queries.shape[0]
    head_width = page_pool.shape[3]
    kv_local = head_width // HD
    group_size = queries.shape[1] // head_width
    capacity = max(2, (REQ_HOST * PAGES_MAX + stores - 1) // stores)
    gathered = lax.all_gather(fresh_kv, "tp", axis=1, tiled=True)
    new_kv = lax.dynamic_slice_in_dim(gathered, lax.axis_index("tp") * head_width, head_width, 2)
    buffer, position = plan_requests(page_host, page_slot, prefix_len, stores, capacity)
    arrived = lax.all_to_all(
        jnp.take(
            page_pool,
            lax.all_to_all(buffer, "store", split_axis=0, concat_axis=0, tiled=True),
            axis=0,
        ),
        "store",
        split_axis=0,
        concat_axis=0,
        tiled=True,
    )
    flat_pages = arrived.reshape(stores * capacity, 2, PAGE, head_width)
    fetched = jnp.take(flat_pages, position, axis=0).reshape(
        REQ_HOST, PAGES_MAX, 2, PAGE, head_width
    )
    lengths = fresh_len[0]
    offsets = jnp.cumsum(lengths) - lengths
    positions = jnp.arange(MOST_NEW, dtype=jnp.int32)
    cache_index = jnp.arange(PAGES_MAX * PAGE, dtype=jnp.int32)
    output = jnp.zeros_like(queries)
    for request in range(REQ_HOST):
        offset = offsets[request]
        length = lengths[request]
        window_start = jnp.minimum(offset, block_rows - MOST_NEW)
        q_rows = lax.dynamic_slice_in_dim(queries, window_start, MOST_NEW, 0).reshape(
            MOST_NEW, kv_local, group_size, HD
        )
        new_rows = lax.dynamic_slice_in_dim(new_kv, window_start, MOST_NEW, 1).reshape(
            2, MOST_NEW, kv_local, HD
        )
        cached_keys = fetched[request, :, 0].reshape(PAGES_MAX * PAGE, kv_local, HD)
        cached_values = fetched[request, :, 1].reshape(PAGES_MAX * PAGE, kv_local, HD)
        key_rows = jnp.concatenate([cached_keys, new_rows[0]], axis=0)
        value_rows = jnp.concatenate([cached_values, new_rows[1]], axis=0)
        query_pos = window_start + positions
        cache_ok = jnp.broadcast_to(
            cache_index[None, :] < prefix_len[request], (MOST_NEW, PAGES_MAX * PAGE)
        )
        fresh_ok = (query_pos[None, :] >= offset) & (query_pos[None, :] <= query_pos[:, None])
        key_valid = jnp.concatenate([cache_ok, fresh_ok], axis=1)
        mixed_rows = attend(q_rows, key_rows, value_rows, key_valid).reshape(
            MOST_NEW, queries.shape[1]
        )
        row_ok = (query_pos >= offset) & (query_pos < offset + length)
        old_rows = lax.dynamic_slice_in_dim(output, window_start, MOST_NEW, 0)
        output = lax.dynamic_update_slice_in_dim(
            output, jnp.where(row_ok[:, None], mixed_rows, old_rows), window_start, 0
        )
    return output


def solution(mesh):
    placed = (
        P("store", "tp"),
        P(None, ("store", "tp"), None),
        P("store", None, None, "tp"),
        P("store", None),
        P("store", None),
        P("store"),
        P("store", None),
    )
    return jax.shard_map(
        local, mesh=mesh, in_specs=placed, out_specs=P("store", "tp"), check_vma=False
    )
```

profile of v0, /device:TPU:2, one launch (start us, length us, event | category | flops | bytes accessed | tf_op | source)
XLA Modules:
  0.0 311.5 jit_solution(1080985737066531450)
XLA Ops:
  9.4 21.1 %all_to_all.20 = s32[32,1,2]{2,1,0:T(1,128)S(1)} all-to-all(s32[32,1,2]{2,1,0:T(1,128)S(1)} %bitcast.273), channel_id=1, replica_groups=mesh['store'=32,'tp'=8] {'store'}, dimensions={0} | all-to-all | bytes 512 | tf_op jit(solution)/shard_map/all_to_all | solution.py:63
  30.9 5.3 %gather_fusion = bf16[64,2,128,128]{3,2,1,0:T(8,128)(2,1)} fusion(bf16[64,2,128,128]{3,2,1,0:T(8,128)(2,1)} %param.9, s32[1024]{0:T(1024)S(1)} %pad_clamp_fusion.1), kind=kCustom, calls=%fused_computation | custom fusion | bytes 8388864 | tf_op jit(solution)/shard_map/jit(_take)/gather | solution.py:61
  36.2 4.5 %broadcast_select_fusion = bf16[32,2,2,128,128]{4,3,2,1,0:T(8,128)(2,1)} fusion(bf16[32,2,2,128,128]{4,3,2,1,0:T(8,128)(2,1)} %bitcast.255, pred[32,2]{1,0:T(8,128)(4,1)S(1)} %copy.87), kind=kLoop, calls=%fused_computation.42 | loop fusion | flops 2097152 | bytes 8388672 | tf_op jit(solution)/shard_map/jit(_take)/select_n | solution.py:61
  40.7 4.9 %all-to-all-start.1 = ((bf16[32,2,2,128,128]{4,3,2,1,0:T(8,128)(2,1)}), bf16[32,2,2,128,128]{4,3,2,1,0:T(8,128)(2,1)}, u32[]{:S(2)}, u32[]{:S(2)}) async-start(bf16[32,2,2,128,128]{4,3,2,1,0:T(8,128)(2,1)} %broadcast_select_fusion), calls=%async_computation.1 | async-start | bytes 8388608 | tf_op jit(solution)/shard_map/all_to_all | solution.py:60
  49.8 2.1 constant_dynamic-slice_fusion
  51.9 2.3 copy.129
  56.3 2.4 copy.128
  72.7 10.4 %all-gather.2.cloned.1.call-done = bf16[2,1024,1024]{2,1,0:T(8,128)(2,1)} async-done(((bf16[2,128,1024]{2,1,0:T(8,128)(2,1)}), bf16[2,1024,1024]{2,1,0:T(8,128)(2,1)}) %all-gather.2.cloned.1.call-update) | async-done | bytes 4194320 | tf_op jit(solution)/shard_map/all_gather | solution.py:57
  83.1 2.8 dynamic-slice_bitcast_fusion.1
  88.9 52.7 %all-to-all-done.1 = bf16[32,2,2,128,128]{4,3,2,1,0:T(8,128)(2,1)} async-done(((bf16[32,2,2,128,128]{4,3,2,1,0:T(8,128)(2,1)}), bf16[32,2,2,128,128]{4,3,2,1,0:T(8,128)(2,1)}, u32[]{:S(2)}, u32[]{:S(2)}) %all-to-all-start.1) | async-done | bytes 4194336 | tf_op jit(solution)/shard_map/all_to_all | solution.py:60
  141.6 4.3 %gather_fusion.1 = bf16[32,2,128,128]{3,2,1,0:T(8,128)(2,1)} fusion(bf16[64,2,128,128]{3,2,1,0:T(8,128)(2,1)} %bitcast.9, s32[1024]{0:T(1024)S(1)} %pad_clamp_fusion), kind=kCustom, calls=%fused_computation.1 | custom fusion | bytes 4194432 | tf_op jit(solution)/shard_map/jit(_take)/gather | solution.py:72
  145.9 1.8 broadcast_select_fusion.1
  150.7 9.9 %fusion = (f32[8,384]{1,0:T(8,128)S(1)}, f32[1408,384,8]{1,0,2:T(8,128)}) fusion(pred[384,1408]{0,1:T(8,128)(4,1)S(1)} %pad_add_fusion.3, bf16[384,8,128]{0,2,1:T(8,128)(2,1)} %bitcast.260, bf16[384,1,128]{2,0,1:T(8,128)(2,1)} %get-tuple-element.9, bf16[1024,1,128]{2,0,1:T(8,128)(2,1)} %bitcast.264), kind=kOutput, calls=%fused_computation.4 | convolution fusion | flops 1120990208 | bytes 19001344 | tf_op jit(solution)/shard_map/mkgd,nkd->kgmn/dot_general | solution.py:37
  160.6 9.8 %fusion.18 = f32[8,384]{1,0:T(8,128)S(1)} fusion(f32[1408,384,8]{1,0,2:T(8,128)} %get-tuple-element.44, f32[8,384]{1,0:T(8,128)S(1)} %get-tuple-element.43, pred[384,1408]{0,1:T(8,128)(4,1)S(1)} %pad_add_fusion.3), kind=kLoop, calls=%fused_computation.28 | loop fusion | flops 17298432 | bytes 17866752 | tf_op jit(solution)/shard_map/reduce_sum | solution.py:42
  170.5 10.7 %fusion.36 = bf16[384,1,8,128]{0,3,2,1:T(8,128)(2,1)} fusion(f32[1408,384,8]{1,0,2:T(8,128)} %get-tuple-element.44, f32[8,384]{1,0:T(8,128)S(1)} %get-tuple-element.43, pred[384,1408]{0,1:T(8,128)(4,1)S(1)} %pad_add_fusion.3, f32[384,8]{0,1:T(8,128)S(1)} %bitcast.274, bf16[384,1,128]{0,2,1:T(8,128)(2,1)} %copy.109, bf16[1024,1,128]{0,2,1:T(8,128)(2,1)} %copy.125), kind=kOutput, calls=%fused_computation.49 | convolution fusion | flops 1126105088 | bytes 19013632 | tf_op jit(solution)/shard_map/kgmn,nkd->mkgd/dot_general | solution.py:44
  181.1 2.3 copy.113
  185.2 9.9 %fusion.3 = (f32[8,384]{1,0:T(8,128)S(1)}, f32[1408,384,8]{1,0,2:T(8,128)}) fusion(pred[384,1408]{0,1:T(8,128)(4,1)S(1)} %pad_add_fusion.2, bf16[384,8,128]{0,2,1:T(8,128)(2,1)} %bitcast.259, bf16[384,1,128]{2,0,1:T(8,128)(2,1)} %get-tuple-element.10, bf16[1024,1,128]{2,0,1:T(8,128)(2,1)} %bitcast.263), kind=kOutput, calls=%fused_computation.9 | convolution fusion | flops 1120990208 | bytes 19001344 | tf_op jit(solution)/shard_map/mkgd,nkd->kgmn/dot_general | solution.py:37
  195.2 9.4 %fusion.16 = f32[8,384]{1,0:T(8,128)S(1)} fusion(f32[1408,384,8]{1,0,2:T(8,128)} %get-tuple-element.42, f32[8,384]{1,0:T(8,128)S(1)} %get-tuple-element.41, pred[384,1408]{0,1:T(8,128)(4,1)S(1)} %pad_add_fusion.2), kind=kLoop, calls=%fused_computation.26 | loop fusion | flops 17298432 | bytes 17866752 | tf_op jit(solution)/shard_map/reduce_sum | solution.py:42
  204.6 10.8 %fusion.37 = bf16[384,1,8,128]{0,3,2,1:T(8,128)(2,1)} fusion(f32[1408,384,8]{1,0,2:T(8,128)} %get-tuple-element.42, f32[8,384]{1,0:T(8,128)S(1)} %get-tuple-element.41, pred[384,1408]{0,1:T(8,128)(4,1)S(1)} %pad_add_fusion.2, f32[384,8]{0,1:T(8,128)S(1)} %bitcast.275, bf16[384,1,128]{0,2,1:T(8,128)(2,1)S(1)} %copy-done.9, bf16[1024,1,128]{0,2,1:T(8,128)(2,1)} %copy.124), kind=kOutput, calls=%fused_computation.51 | convolution fusion | flops 1126105088 | bytes 19013632 | tf_op jit(solution)/shard_map/kgmn,nkd->mkgd/dot_general | solution.py:44
  215.4 2.3 copy.107
  218.6 8.9 %fusion.6 = (f32[8,384]{1,0:T(8,128)S(1)}, f32[1408,384,8]{1,0,2:T(8,128)}) fusion(pred[384,1408]{0,1:T(8,128)(4,1)S(1)} %pad_add_fusion.1, bf16[384,8,128]{0,2,1:T(8,128)(2,1)} %bitcast.258, bf16[384,1,128]{2,0,1:T(8,128)(2,1)S(1)} %copy-done.6, bf16[1024,1,128]{2,0,1:T(8,128)(2,1)S(1)} %bitcast.262), kind=kOutput, calls=%fused_computation.14 | convolution fusion | flops 1120990208 | bytes 19001344 | tf_op jit(solution)/shard_map/mkgd,nkd->kgmn/dot_general | solution.py:37
  227.5 9.5 %fusion.14 = f32[8,384]{1,0:T(8,128)S(1)} fusion(f32[1408,384,8]{1,0,2:T(8,128)} %get-tuple-element.40, f32[8,384]{1,0:T(8,128)S(1)} %get-tuple-element.39, pred[384,1408]{0,1:T(8,128)(4,1)S(1)} %pad_add_fusion.1), kind=kLoop, calls=%fused_computation.24 | loop fusion | flops 17298432 | bytes 17866752 | tf_op jit(solution)/shard_map/reduce_sum | solution.py:42
  237.0 9.7 %fusion.38 = bf16[384,1,8,128]{0,3,2,1:T(8,128)(2,1)S(1)} fusion(f32[1408,384,8]{1,0,2:T(8,128)} %get-tuple-element.40, f32[8,384]{1,0:T(8,128)S(1)} %get-tuple-element.39, pred[384,1408]{0,1:T(8,128)(4,1)S(1)} %pad_add_fusion.1, f32[384,8]{0,1:T(8,128)S(1)} %bitcast.276, bf16[384,1,128]{0,2,1:T(8,128)(2,1)S(1)} %copy-done.8, bf16[1024,1,128]{0,2,1:T(8,128)(2,1)} %copy.123), kind=kOutput, calls=%fused_computation.53 | convolution fusion | flops 1126105088 | bytes 19013632 | tf_op jit(solution)/shard_map/kgmn,nkd->mkgd/dot_general | solution.py:44
  248.1 7.9 %fusion.9 = (f32[8,384]{1,0:T(8,128)S(1)}, f32[1408,384,8]{1,0,2:T(8,128)}) fusion(pred[384,1408]{0,1:T(8,128)(4,1)S(1)} %pad_add_fusion, bf16[384,8,128]{0,2,1:T(8,128)(2,1)S(1)} %bitcast.257, bf16[384,1,128]{2,0,1:T(8,128)(2,1)S(1)} %copy-done.5, bf16[1024,1,128]{2,0,1:T(8,128)(2,1)S(1)} %bitcast.261), kind=kOutput, calls=%fused_computation.19 | convolution fusion | flops 1120990208 | bytes 19001344 | tf_op jit(solution)/shard_map/mkgd,nkd->kgmn/dot_general | solution.py:37
  256.0 9.4 %fusion.12 = f32[8,384]{1,0:T(8,128)S(1)} fusion(f32[1408,384,8]{1,0,2:T(8,128)} %get-tuple-element.38, f32[8,384]{1,0:T(8,128)S(1)} %get-tuple-element.37, pred[384,1408]{0,1:T(8,128)(4,1)S(1)} %pad_add_fusion), kind=kLoop, calls=%fused_computation.22 | loop fusion | flops 17298432 | bytes 17866752 | tf_op jit(solution)/shard_map/reduce_sum | solution.py:42
  265.5 9.7 %fusion.39 = bf16[384,1,8,128]{0,3,2,1:T(8,128)(2,1)S(1)} fusion(f32[1408,384,8]{1,0,2:T(8,128)} %get-tuple-element.38, f32[8,384]{1,0:T(8,128)S(1)} %get-tuple-element.37, pred[384,1408]{0,1:T(8,128)(4,1)S(1)} %pad_add_fusion, f32[384,8]{0,1:T(8,128)S(1)} %bitcast.277, bf16[384,1,128]{0,2,1:T(8,128)(2,1)S(1)} %copy-done.7, bf16[1024,1,128]{0,2,1:T(8,128)(2,1)S(1)} %copy.122), kind=kOutput, calls=%fused_computation.55 | convolution fusion | flops 1126105088 | bytes 19013632 | tf_op jit(solution)/shard_map/kgmn,nkd->mkgd/dot_general | solution.py:44
  276.7 5.6 %dynamic_update_slice.12 = bf16[1024,1024]{1,0:T(8,128)(2,1)S(1)} dynamic-update-slice(bf16[1024,1024]{1,0:T(8,128)(2,1)S(1)} %broadcast_in_dim.152, bf16[384,1024]{1,0:T(8,128)(2,1)} %broadcast_select_fusion.2, s32[]{:T(128)S(6)} %select_n.157, s32[]{:T(128)} %constant.116.clone.1) | dynamic-update-slice | bytes 1572868 | tf_op jit(solution)/shard_map/dynamic_update_slice | solution.py:105
  282.3 2.3 dynamic-slice_select_fusion.2
  284.7 5.5 %dynamic_update_slice.13 = bf16[1024,1024]{1,0:T(8,128)(2,1)S(1)} dynamic-update-slice(bf16[1024,1024]{1,0:T(8,128)(2,1)S(1)} %dynamic_update_slice.12, bf16[384,1024]{1,0:T(8,128)(2,1)} %dynamic-slice_select_fusion.2, s32[]{:T(128)S(6)} %select_n.164, s32[]{:T(128)} %constant.116.clone.1) | dynamic-update-slice | bytes 1572868 | tf_op jit(solution)/shard_map/dynamic_update_slice | solution.py:105
  290.2 2.3 dynamic-slice_select_fusion.1
  292.6 5.5 %dynamic_update_slice.14 = bf16[1024,1024]{1,0:T(8,128)(2,1)S(1)} dynamic-update-slice(bf16[1024,1024]{1,0:T(8,128)(2,1)S(1)} %dynamic_update_slice.13, bf16[384,1024]{1,0:T(8,128)(2,1)} %dynamic-slice_select_fusion.1, s32[]{:T(128)S(6)} %select_n.169, s32[]{:T(128)} %constant.116.clone.1) | dynamic-update-slice | bytes 1572868 | tf_op jit(solution)/shard_map/dynamic_update_slice | solution.py:105
  299.7 4.7 %dynamic_update_slice.15 = bf16[1024,1024]{1,0:T(8,128)(2,1)} dynamic-update-slice(bf16[1024,1024]{1,0:T(8,128)(2,1)} %copy-done, bf16[384,1024]{1,0:T(8,128)(2,1)} %dynamic-slice_select_fusion, s32[]{:T(128)S(6)} %select_n.174, s32[]{:T(128)} %constant.116.clone.1) | dynamic-update-slice | bytes 1572868 | tf_op jit(solution)/shard_map/dynamic_update_slice | solution.py:105
  (96 shorter events, 29.1 us)
Async XLA Ops:
  6.5 47.7 %copy-start.10 = (s32[4,8]{1,0:T(4,128)S(1)}, s32[4,8]{1,0:T(4,128)}, u32[]{:S(2)}) copy-start(s32[4,8]{1,0:T(4,128)} %param.10) | copy-start | bytes 388
  6.5 39.8 %copy-start.11 = (s32[1,4]{1,0:T(1,128)S(1)}, s32[1,4]{1,0:T(1,128)}, u32[]{:S(2)}) copy-start(s32[1,4]{1,0:T(1,128)} %param.13) | copy-start | bytes 52
  6.5 43.3 %copy-start.1 = (bf16[1024,1024]{1,0:T(8,128)(2,1)S(1)}, bf16[1024,1024]{1,0:T(8,128)(2,1)}, u32[]{:S(2)}) copy-start(bf16[1024,1024]{1,0:T(8,128)(2,1)} %param.7) | copy-start | bytes 6291460
  30.9 28.9 %copy-start.12 = (s32[4]{0:T(128)S(1)}, s32[4]{0:T(128)}, u32[]{:S(2)}) copy-start(s32[4]{0:T(128)} %param.12) | copy-start | bytes 52
  40.7 100.9 %all-to-all-start.1 = ((bf16[32,2,2,128,128]{4,3,2,1,0:T(8,128)(2,1)}), bf16[32,2,2,128,128]{4,3,2,1,0:T(8,128)(2,1)}, u32[]{:S(2)}, u32[]{:S(2)}) async-start(bf16[32,2,2,128,128]{4,3,2,1,0:T(8,128)(2,1)} %broadcast_select_fusion), calls=%async_computation.1 | async-start | bytes 8388608 | tf_op jit(solution)/shard_map/all_to_all | solution.py:60
  45.6 37.5 %all-gather.2.cloned.1.call-start = ((), (), s32[]{:S(2)}) async-start(), calls=%async_computation.2 | async-start | bytes 4718592 | tf_op jit(solution)/shard_map/all_gather | solution.py:57
  185.2 19.4 %copy-start.9 = (bf16[384,1,128]{0,2,1:T(8,128)(2,1)S(1)}, bf16[384,1,128]{0,2,1:T(8,128)(2,1)}, u32[]{:S(2)}) copy-start(bf16[384,1,128]{0,2,1:T(8,128)(2,1)} %copy.103) | copy-start | bytes 294916
  204.6 13.2 %copy-start.4 = (bf16[1,8,1,128,128]{4,3,2,1,0:T(8,128)(2,1)S(1)}, bf16[1,8,1,128,128]{4,3,2,1,0:T(8,128)(2,1)}, u32[]{:S(2)}) copy-start(bf16[1,8,1,128,128]{4,3,2,1,0:T(8,128)(2,1)} %get-tuple-element.18) | copy-start | bytes 786436
  204.6 14.0 %copy-start.6 = (bf16[384,1,128]{2,0,1:T(8,128)(2,1)S(1)}, bf16[384,1,128]{2,0,1:T(8,128)(2,1)}, u32[]{:S(2)}) copy-start(bf16[384,1,128]{2,0,1:T(8,128)(2,1)} %get-tuple-element.11) | copy-start | bytes 294916
  227.5 9.5 %copy-start.8 = (bf16[384,1,128]{0,2,1:T(8,128)(2,1)S(1)}, bf16[384,1,128]{0,2,1:T(8,128)(2,1)}, u32[]{:S(2)}) copy-start(bf16[384,1,128]{0,2,1:T(8,128)(2,1)} %copy.97) | copy-start | bytes 294916
  237.0 11.0 %copy-start.3 = (bf16[1,8,1,128,128]{4,3,2,1,0:T(8,128)(2,1)S(1)}, bf16[1,8,1,128,128]{4,3,2,1,0:T(8,128)(2,1)}, u32[]{:S(2)}) copy-start(bf16[1,8,1,128,128]{4,3,2,1,0:T(8,128)(2,1)} %get-tuple-element.20) | copy-start | bytes 786436
  237.0 11.1 %copy-start.5 = (bf16[384,1,128]{2,0,1:T(8,128)(2,1)S(1)}, bf16[384,1,128]{2,0,1:T(8,128)(2,1)}, u32[]{:S(2)}) copy-start(bf16[384,1,128]{2,0,1:T(8,128)(2,1)} %get-tuple-element.12) | copy-start | bytes 294916
  248.1 17.4 %copy-start.7 = (bf16[384,1,128]{0,2,1:T(8,128)(2,1)S(1)}, bf16[384,1,128]{0,2,1:T(8,128)(2,1)}, u32[]{:S(2)}) copy-start(bf16[384,1,128]{0,2,1:T(8,128)(2,1)} %copy.91) | copy-start | bytes 294916
  265.5 32.7 %copy-start.2 = (bf16[384,1024]{1,0:T(8,128)(2,1)S(1)}, bf16[384,1024]{1,0:T(8,128)(2,1)}, u32[]{:S(2)}) copy-start(bf16[384,1024]{1,0:T(8,128)(2,1)} %copy.113) | copy-start | bytes 2359300
  298.1 1.6 copy-start
Sparse Core Ops, SparseCore 0:
  48.3 34.8 all-gather.1
where the time goes:
time: 315 us; the launch traced here: 311 us
  matrix products  77.5 us (25%)
  waiting for transfers between devices  63.6 us (20%)
  local copies, waits for them, and re-layouts  62.7 us (20%)
  other arithmetic  60 us (19%)
  between operations  21.5 us (7%)
  blocking collectives  21.1 us (7%)
  starting transfers between devices  5.07 us (2%)
    all_to_all x1, waiting for transfers between devices, local(): lax.all_to_all(jnp.take(page_pool, lax.all_to_all(buffer, 'store', split_...  52.7 us
    dot_general x4, matrix products, attend(): jnp.einsum('kgmn,nkd->mkgd', rounded, value_rows, preferred_element_type=...  40.9 us
    reduce_sum x4, other arithmetic, attend(): row_total = jnp.sum(weights, axis=-1)  38.1 us
    dot_general x4, matrix products, attend(): jnp.einsum('mkgd,nkd->kgmn', q_rows, key_rows, preferred_element_type=jnp...  36.7 us
    dynamic_update_slice x4, local copies, waits for them, and re-layouts, local(): lax.dynamic_update_slice_in_dim(output, jnp.where(row_ok[:, None], mixed_...  21.4 us
    all_to_all x1, blocking collectives, local(): lax.all_to_all(buffer, 'store', split_axis=0, concat_axis=0, tiled=True)  21.1 us
    all_gather x1, waiting for transfers between devices, local(): gathered = lax.all_gather(fresh_kv, 'tp', axis=1, tiled=True)  10.4 us
    unnamed x30, local copies, waits for them, and re-layouts  7.46 us
  transfers between devices with their start and end apart: 2, of which 2 were waited for; matrix products, arithmetic and copies ran while one was open for 8% of the time, Pallas kernels for 0%

commit v1 on v0

--- a/solution.py
+++ b/solution.py
@@ -1,3 +1,4 @@
+import functools
 import math
 import jax
 import jax.numpy as jnp
@@ -9,6 +10,22 @@
 PAGE = 128
 PAGES_MAX = 8
 MOST_NEW = 384
+
+
+def _render_series(payload, along_axis):
+    mid_arr = jnp.concatenate(
+        jax.lax.all_to_all(
+            jnp.stack(tuple((payload for _ in range(jax.lax.axis_size(along_axis))))),
+            split_axis=0,
+            axis_name=along_axis,
+            concat_axis=0,
+        ),
+        axis=1,
+    )
+    return mid_arr
+
+
+wrap_strings_by_axis = functools.partial(_render_series, along_axis="tp")
 
 
 def plan_requests(owners, slot_ids, prefix, stores, capacity):
@@ -54,7 +71,7 @@
     kv_local = head_width // HD
     group_size = queries.shape[1] // head_width
     capacity = max(2, (REQ_HOST * PAGES_MAX + stores - 1) // stores)
-    gathered = lax.all_gather(fresh_kv, "tp", axis=1, tiled=True)
+    gathered = wrap_strings_by_axis(fresh_kv)
     new_kv = lax.dynamic_slice_in_dim(gathered, lax.axis_index("tp") * head_width, head_width, 2)
     buffer, position = plan_requests(page_host, page_slot, prefix_len, stores, capacity)
     arrived = lax.all_to_all(

time: 315 us -> 350 us (1.11)
  waiting for transfers between devices: 63.6 us -> 102 us
  between operations: 21.5 us -> 8.03 us
  starting transfers between devices: 5.07 us -> 10.2 us
  local copies, waits for them, and re-layouts: 62.7 us -> 67.6 us
    all_to_all x0 -> x1, waiting for transfers between devices: none -> 38.1 us  [_render_series(): jax.lax.all_to_all(jnp.stack(tuple((payload for _ in range(jax.lax.axis_s...]
    all_to_all x1, waiting for transfers between devices: 52.7 us -> 63.6 us  [local(): lax.all_to_all(jnp.take(page_pool, lax.all_to_all(buffer, 'store', split_...]
    all_gather x1 -> x0, waiting for transfers between devices: 10.4 us -> none  [local(): gathered = lax.all_gather(fresh_kv, 'tp', axis=1, tiled=True)]
    all_to_all x0 -> x1, starting transfers between devices: none -> 5.15 us  [_render_series(): jax.lax.all_to_all(jnp.stack(tuple((payload for _ in range(jax.lax.axis_s...]
    another operation x0 -> x1, local copies, waits for them, and re-layouts: none -> 3.55 us  [_render_series(): jnp.stack(tuple((payload for _ in range(jax.lax.axis_size(along_axis)))))]
  transfers between devices with their start and end apart: 2 -> 2, of which waited for: 2 -> 2; matrix products, arithmetic and copies ran while one was open for 8% -> 10% of each run, Pallas kernels for 0% -> 0%
where the time goes in v1:
time: 350 us; the launch traced here: 346 us
  waiting for transfers between devices  102 us (29%)
  matrix products  77.7 us (22%)
  local copies, waits for them, and re-layouts  67.6 us (19%)
  other arithmetic  59.6 us (17%)
  blocking collectives  21.1 us (6%)
  starting transfers between devices  10.2 us (3%)
  between operations  8.03 us (2%)
    all_to_all x1, waiting for transfers between devices, local(): lax.all_to_all(jnp.take(page_pool, lax.all_to_all(buffer, 'store', split_...  63.6 us
    dot_general x4, matrix products, attend(): jnp.einsum('kgmn,nkd->mkgd', rounded, value_rows, preferred_element_type=...  41.1 us
    all_to_all x1, waiting for transfers between devices, _render_series(): jax.lax.all_to_all(jnp.stack(tuple((payload for _ in range(jax.lax.axis_s...  38.1 us
    reduce_sum x4, other arithmetic, attend(): row_total = jnp.sum(weights, axis=-1)  37.9 us
    dot_general x4, matrix products, attend(): jnp.einsum('mkgd,nkd->kgmn', q_rows, key_rows, preferred_element_type=jnp...  36.6 us
    dynamic_update_slice x4, local copies, waits for them, and re-layouts, local(): lax.dynamic_update_slice_in_dim(output, jnp.where(row_ok[:, None], mixed_...  21.4 us
    all_to_all x1, blocking collectives, local(): lax.all_to_all(buffer, 'store', split_axis=0, concat_axis=0, tiled=True)  21.1 us
    unnamed x30, local copies, waits for them, and re-layouts  7.46 us
  transfers between devices with their start and end apart: 2, of which 2 were waited for; matrix products, arithmetic and copies ran while one was open for 10% of the time, Pallas kernels for 0%

profile of v1, /device:TPU:2, one launch (start us, length us, event | category | flops | bytes accessed | tf_op | source)
XLA Modules:
  0.0 345.9 jit_solution(2673775640052587035)
XLA Ops:
  2.8 21.1 %all_to_all.25 = s32[32,1,2]{2,1,0:T(1,128)S(1)} all-to-all(s32[32,1,2]{2,1,0:T(1,128)S(1)} %bitcast.276), channel_id=1, replica_groups=mesh['store'=32,'tp'=8] {'store'}, dimensions={0} | all-to-all | bytes 512 | tf_op jit(solution)/shard_map/all_to_all | solution.py:80
  23.8 3.5 %stack.2 = bf16[8,2,128,1024]{3,2,1,0:T(8,128)(2,1)} broadcast(bf16[2,128,1024]{2,1,0:T(8,128)(2,1)} %param.8), dimensions={1,2,3} | broadcast | bytes 4718592 | tf_op jit(solution)/shard_map/stack | solution.py:18
  27.4 5.1 %all-to-all-start.2 = ((bf16[8,2,128,1024]{3,2,1,0:T(8,128)(2,1)}), bf16[8,2,128,1024]{3,2,1,0:T(8,128)(2,1)}, u32[]{:S(2)}, u32[]{:S(2)}) async-start(bf16[8,2,128,1024]{3,2,1,0:T(8,128)(2,1)} %stack.2), calls=%async_computation.2 | async-start | bytes 8388608 | tf_op jit(solution)/shard_map/all_to_all | solution.py:17
  33.0 5.2 %gather_fusion = bf16[64,2,128,128]{3,2,1,0:T(8,128)(2,1)} fusion(bf16[64,2,128,128]{3,2,1,0:T(8,128)(2,1)} %param.9, s32[1024]{0:T(1024)S(1)} %pad_clamp_fusion.1), kind=kCustom, calls=%fused_computation | custom fusion | bytes 8388864 | tf_op jit(solution)/shard_map/jit(_take)/gather | solution.py:78
  38.2 4.5 %broadcast_select_fusion = bf16[32,2,2,128,128]{4,3,2,1,0:T(8,128)(2,1)} fusion(bf16[32,2,2,128,128]{4,3,2,1,0:T(8,128)(2,1)} %bitcast.257, pred[32,2]{1,0:T(8,128)(4,1)S(1)} %copy.88), kind=kLoop, calls=%fused_computation.42 | loop fusion | flops 2097152 | bytes 8388672 | tf_op jit(solution)/shard_map/jit(_take)/select_n | solution.py:78
  42.7 38.1 %all-to-all-done.2 = bf16[8,2,128,1024]{3,2,1,0:T(8,128)(2,1)} async-done(((bf16[8,2,128,1024]{3,2,1,0:T(8,128)(2,1)}), bf16[8,2,128,1024]{3,2,1,0:T(8,128)(2,1)}, u32[]{:S(2)}, u32[]{:S(2)}) %all-to-all-start.2) | async-done | bytes 4194336 | tf_op jit(solution)/shard_map/all_to_all | solution.py:17
  80.9 5.0 %all-to-all-start.1 = ((bf16[32,2,2,128,128]{4,3,2,1,0:T(8,128)(2,1)}), bf16[32,2,2,128,128]{4,3,2,1,0:T(8,128)(2,1)}, u32[]{:S(2)}, u32[]{:S(2)}) async-start(bf16[32,2,2,128,128]{4,3,2,1,0:T(8,128)(2,1)} %broadcast_select_fusion), calls=%async_computation.1 | async-start | bytes 8388608 | tf_op jit(solution)/shard_map/all_to_all | solution.py:77
  91.5 2.3 copy.131
  95.8 2.4 copy.130
  112.3 2.6 copy.92
  119.3 63.6 %all-to-all-done.1 = bf16[32,2,2,128,128]{4,3,2,1,0:T(8,128)(2,1)} async-done(((bf16[32,2,2,128,128]{4,3,2,1,0:T(8,128)(2,1)}), bf16[32,2,2,128,128]{4,3,2,1,0:T(8,128)(2,1)}, u32[]{:S(2)}, u32[]{:S(2)}) %all-to-all-start.1) | async-done | bytes 4194336 | tf_op jit(solution)/shard_map/all_to_all | solution.py:77
  182.9 4.3 %gather_fusion.1 = bf16[32,2,128,128]{3,2,1,0:T(8,128)(2,1)} fusion(bf16[64,2,128,128]{3,2,1,0:T(8,128)(2,1)} %bitcast.9, s32[1024]{0:T(1024)S(1)} %pad_clamp_fusion), kind=kCustom, calls=%fused_computation.1 | custom fusion | bytes 4194432 | tf_op jit(solution)/shard_map/jit(_take)/gather | solution.py:89
  192.0 9.9 %fusion = (f32[8,384]{1,0:T(8,128)S(1)}, f32[1408,384,8]{1,0,2:T(8,128)}) fusion(pred[384,1408]{0,1:T(8,128)(4,1)S(1)} %pad_add_fusion.3, bf16[384,8,128]{0,2,1:T(8,128)(2,1)} %bitcast.263, bf16[384,1,128]{2,0,1:T(8,128)(2,1)} %get-tuple-element.9, bf16[1024,1,128]{2,0,1:T(8,128)(2,1)} %bitcast.267), kind=kOutput, calls=%fused_computation.4 | convolution fusion | flops 1120990208 | bytes 19001344 | tf_op jit(solution)/shard_map/mkgd,nkd->kgmn/dot_general | solution.py:54
  201.9 9.6 %fusion.18 = f32[8,384]{1,0:T(8,128)S(1)} fusion(f32[1408,384,8]{1,0,2:T(8,128)} %get-tuple-element.44, f32[8,384]{1,0:T(8,128)S(1)} %get-tuple-element.43, pred[384,1408]{0,1:T(8,128)(4,1)S(1)} %pad_add_fusion.3), kind=kLoop, calls=%fused_computation.28 | loop fusion | flops 17298432 | bytes 17866752 | tf_op jit(solution)/shard_map/reduce_sum | solution.py:59
  211.6 10.7 %fusion.36 = bf16[384,1,8,128]{0,3,2,1:T(8,128)(2,1)} fusion(f32[1408,384,8]{1,0,2:T(8,128)} %get-tuple-element.44, f32[8,384]{1,0:T(8,128)S(1)} %get-tuple-element.43, pred[384,1408]{0,1:T(8,128)(4,1)S(1)} %pad_add_fusion.3, f32[384,8]{0,1:T(8,128)S(1)} %bitcast.277, bf16[384,1,128]{0,2,1:T(8,128)(2,1)} %copy.111, bf16[1024,1,128]{0,2,1:T(8,128)(2,1)} %copy.127), kind=kOutput, calls=%fused_computation.49 | convolution fusion | flops 1126105088 | bytes 19013632 | tf_op jit(solution)/shard_map/kgmn,nkd->mkgd/dot_general | solution.py:61
  222.2 2.3 copy.115
  226.3 9.9 %fusion.3 = (f32[8,384]{1,0:T(8,128)S(1)}, f32[1408,384,8]{1,0,2:T(8,128)}) fusion(pred[384,1408]{0,1:T(8,128)(4,1)S(1)} %pad_add_fusion.2, bf16[384,8,128]{0,2,1:T(8,128)(2,1)} %bitcast.262, bf16[384,1,128]{2,0,1:T(8,128)(2,1)} %get-tuple-element.10, bf16[1024,1,128]{2,0,1:T(8,128)(2,1)} %bitcast.266), kind=kOutput, calls=%fused_computation.9 | convolution fusion | flops 1120990208 | bytes 19001344 | tf_op jit(solution)/shard_map/mkgd,nkd->kgmn/dot_general | solution.py:54
  236.3 9.4 %fusion.16 = f32[8,384]{1,0:T(8,128)S(1)} fusion(f32[1408,384,8]{1,0,2:T(8,128)} %get-tuple-element.42, f32[8,384]{1,0:T(8,128)S(1)} %get-tuple-element.41, pred[384,1408]{0,1:T(8,128)(4,1)S(1)} %pad_add_fusion.2), kind=kLoop, calls=%fused_computation.26 | loop fusion | flops 17298432 | bytes 17866752 | tf_op jit(solution)/shard_map/reduce_sum | solution.py:59
  245.7 11.0 %fusion.37 = bf16[384,1,8,128]{0,3,2,1:T(8,128)(2,1)} fusion(f32[1408,384,8]{1,0,2:T(8,128)} %get-tuple-element.42, f32[8,384]{1,0:T(8,128)S(1)} %get-tuple-element.41, pred[384,1408]{0,1:T(8,128)(4,1)S(1)} %pad_add_fusion.2, f32[384,8]{0,1:T(8,128)S(1)} %bitcast.278, bf16[384,1,128]{0,2,1:T(8,128)(2,1)S(1)} %copy-done.9, bf16[1024,1,128]{0,2,1:T(8,128)(2,1)} %copy.126), kind=kOutput, calls=%fused_computation.51 | convolution fusion | flops 1126105088 | bytes 19013632 | tf_op jit(solution)/shard_map/kgmn,nkd->mkgd/dot_general | solution.py:61
  256.8 2.3 copy.109
  260.0 8.9 %fusion.6 = (f32[8,384]{1,0:T(8,128)S(1)}, f32[1408,384,8]{1,0,2:T(8,128)}) fusion(pred[384,1408]{0,1:T(8,128)(4,1)S(1)} %pad_add_fusion.1, bf16[384,8,128]{0,2,1:T(8,128)(2,1)} %bitcast.261, bf16[384,1,128]{2,0,1:T(8,128)(2,1)S(1)} %copy-done.6, bf16[1024,1,128]{2,0,1:T(8,128)(2,1)S(1)} %bitcast.265), kind=kOutput, calls=%fused_computation.14 | convolution fusion | flops 1120990208 | bytes 19001344 | tf_op jit(solution)/shard_map/mkgd,nkd->kgmn/dot_general | solution.py:54
  268.8 9.5 %fusion.14 = f32[8,384]{1,0:T(8,128)S(1)} fusion(f32[1408,384,8]{1,0,2:T(8,128)} %get-tuple-element.40, f32[8,384]{1,0:T(8,128)S(1)} %get-tuple-element.39, pred[384,1408]{0,1:T(8,128)(4,1)S(1)} %pad_add_fusion.1), kind=kLoop, calls=%fused_computation.24 | loop fusion | flops 17298432 | bytes 17866752 | tf_op jit(solution)/shard_map/reduce_sum | solution.py:59
  278.3 9.7 %fusion.38 = bf16[384,1,8,128]{0,3,2,1:T(8,128)(2,1)S(1)} fusion(f32[1408,384,8]{1,0,2:T(8,128)} %get-tuple-element.40, f32[8,384]{1,0:T(8,128)S(1)} %get-tuple-element.39, pred[384,1408]{0,1:T(8,128)(4,1)S(1)} %pad_add_fusion.1, f32[384,8]{0,1:T(8,128)S(1)} %bitcast.279, bf16[384,1,128]{0,2,1:T(8,128)(2,1)S(1)} %copy-done.8, bf16[1024,1,128]{0,2,1:T(8,128)(2,1)} %copy.125), kind=kOutput, calls=%fused_computation.53 | convolution fusion | flops 1126105088 | bytes 19013632 | tf_op jit(solution)/shard_map/kgmn,nkd->mkgd/dot_general | solution.py:61
  289.4 7.9 %fusion.9 = (f32[8,384]{1,0:T(8,128)S(1)}, f32[1408,384,8]{1,0,2:T(8,128)}) fusion(pred[384,1408]{0,1:T(8,128)(4,1)S(1)} %pad_add_fusion, bf16[384,8,128]{0,2,1:T(8,128)(2,1)S(1)} %bitcast.260, bf16[384,1,128]{2,0,1:T(8,128)(2,1)S(1)} %copy-done.5, bf16[1024,1,128]{2,0,1:T(8,128)(2,1)S(1)} %bitcast.264), kind=kOutput, calls=%fused_computation.19 | convolution fusion | flops 1120990208 | bytes 19001344 | tf_op jit(solution)/shard_map/mkgd,nkd->kgmn/dot_general | solution.py:54
  297.4 9.4 %fusion.12 = f32[8,384]{1,0:T(8,128)S(1)} fusion(f32[1408,384,8]{1,0,2:T(8,128)} %get-tuple-element.38, f32[8,384]{1,0:T(8,128)S(1)} %get-tuple-element.37, pred[384,1408]{0,1:T(8,128)(4,1)S(1)} %pad_add_fusion), kind=kLoop, calls=%fused_computation.22 | loop fusion | flops 17298432 | bytes 17866752 | tf_op jit(solution)/shard_map/reduce_sum | solution.py:59
  306.8 9.7 %fusion.39 = bf16[384,1,8,128]{0,3,2,1:T(8,128)(2,1)S(1)} fusion(f32[1408,384,8]{1,0,2:T(8,128)} %get-tuple-element.38, f32[8,384]{1,0:T(8,128)S(1)} %get-tuple-element.37, pred[384,1408]{0,1:T(8,128)(4,1)S(1)} %pad_add_fusion, f32[384,8]{0,1:T(8,128)S(1)} %bitcast.280, bf16[384,1,128]{0,2,1:T(8,128)(2,1)S(1)} %copy-done.7, bf16[1024,1,128]{0,2,1:T(8,128)(2,1)S(1)} %copy.124), kind=kOutput, calls=%fused_computation.55 | convolution fusion | flops 1126105088 | bytes 19013632 | tf_op jit(solution)/shard_map/kgmn,nkd->mkgd/dot_general | solution.py:61
  318.0 5.6 %dynamic_update_slice.12 = bf16[1024,1024]{1,0:T(8,128)(2,1)S(1)} dynamic-update-slice(bf16[1024,1024]{1,0:T(8,128)(2,1)S(1)} %broadcast_in_dim.152, bf16[384,1024]{1,0:T(8,128)(2,1)} %broadcast_select_fusion.2, s32[]{:T(128)S(6)} %select_n.157, s32[]{:T(128)} %constant.116.clone.1) | dynamic-update-slice | bytes 1572868 | tf_op jit(solution)/shard_map/dynamic_update_slice | solution.py:122
  323.6 2.3 dynamic-slice_select_fusion.2
  326.0 5.5 %dynamic_update_slice.13 = bf16[1024,1024]{1,0:T(8,128)(2,1)S(1)} dynamic-update-slice(bf16[1024,1024]{1,0:T(8,128)(2,1)S(1)} %dynamic_update_slice.12, bf16[384,1024]{1,0:T(8,128)(2,1)} %dynamic-slice_select_fusion.2, s32[]{:T(128)S(6)} %select_n.164, s32[]{:T(128)} %constant.116.clone.1) | dynamic-update-slice | bytes 1572868 | tf_op jit(solution)/shard_map/dynamic_update_slice | solution.py:122
  331.5 2.3 dynamic-slice_select_fusion.1
  333.9 5.5 %dynamic_update_slice.14 = bf16[1024,1024]{1,0:T(8,128)(2,1)S(1)} dynamic-update-slice(bf16[1024,1024]{1,0:T(8,128)(2,1)S(1)} %dynamic_update_slice.13, bf16[384,1024]{1,0:T(8,128)(2,1)} %dynamic-slice_select_fusion.1, s32[]{:T(128)S(6)} %select_n.169, s32[]{:T(128)} %constant.116.clone.1) | dynamic-update-slice | bytes 1572868 | tf_op jit(solution)/shard_map/dynamic_update_slice | solution.py:122
  341.0 4.7 %dynamic_update_slice.15 = bf16[1024,1024]{1,0:T(8,128)(2,1)} dynamic-update-slice(bf16[1024,1024]{1,0:T(8,128)(2,1)} %copy-done, bf16[384,1024]{1,0:T(8,128)(2,1)} %dynamic-slice_select_fusion, s32[]{:T(128)S(6)} %select_n.174, s32[]{:T(128)} %constant.116.clone.1) | dynamic-update-slice | bytes 1572868 | tf_op jit(solution)/shard_map/dynamic_update_slice | solution.py:122
  (97 shorter events, 33.6 us)
Async XLA Ops:
  27.4 58.5 %copy-start.11 = (s32[1,4]{1,0:T(1,128)S(1)}, s32[1,4]{1,0:T(1,128)}, u32[]{:S(2)}) copy-start(s32[1,4]{1,0:T(1,128)} %param.13) | copy-start | bytes 52
  27.4 62.0 %copy-start.1 = (bf16[1024,1024]{1,0:T(8,128)(2,1)S(1)}, bf16[1024,1024]{1,0:T(8,128)(2,1)}, u32[]{:S(2)}) copy-start(bf16[1024,1024]{1,0:T(8,128)(2,1)} %param.7) | copy-start | bytes 6291460
  27.4 53.5 %all-to-all-start.2 = ((bf16[8,2,128,1024]{3,2,1,0:T(8,128)(2,1)}), bf16[8,2,128,1024]{3,2,1,0:T(8,128)(2,1)}, u32[]{:S(2)}, u32[]{:S(2)}) async-start(bf16[8,2,128,1024]{3,2,1,0:T(8,128)(2,1)} %stack.2), calls=%async_computation.2 | async-start | bytes 8388608 | tf_op jit(solution)/shard_map/all_to_all | solution.py:17
  32.5 61.3 %copy-start.10 = (s32[4,8]{1,0:T(4,128)S(1)}, s32[4,8]{1,0:T(4,128)}, u32[]{:S(2)}) copy-start(s32[4,8]{1,0:T(4,128)} %param.10) | copy-start | bytes 388
  32.9 66.5 %copy-start.12 = (s32[4]{0:T(128)S(1)}, s32[4]{0:T(128)}, u32[]{:S(2)}) copy-start(s32[4]{0:T(128)} %param.12) | copy-start | bytes 52
  80.9 102.0 %all-to-all-start.1 = ((bf16[32,2,2,128,128]{4,3,2,1,0:T(8,128)(2,1)}), bf16[32,2,2,128,128]{4,3,2,1,0:T(8,128)(2,1)}, u32[]{:S(2)}, u32[]{:S(2)}) async-start(bf16[32,2,2,128,128]{4,3,2,1,0:T(8,128)(2,1)} %broadcast_select_fusion), calls=%async_computation.1 | async-start | bytes 8388608 | tf_op jit(solution)/shard_map/all_to_all | solution.py:77
  226.3 19.4 %copy-start.9 = (bf16[384,1,128]{0,2,1:T(8,128)(2,1)S(1)}, bf16[384,1,128]{0,2,1:T(8,128)(2,1)}, u32[]{:S(2)}) copy-start(bf16[384,1,128]{0,2,1:T(8,128)(2,1)} %copy.105) | copy-start | bytes 294916
  245.7 13.4 %copy-start.4 = (bf16[1,8,1,128,128]{4,3,2,1,0:T(8,128)(2,1)S(1)}, bf16[1,8,1,128,128]{4,3,2,1,0:T(8,128)(2,1)}, u32[]{:S(2)}) copy-start(bf16[1,8,1,128,128]{4,3,2,1,0:T(8,128)(2,1)} %get-tuple-element.18) | copy-start | bytes 786436
  245.7 14.3 %copy-start.6 = (bf16[384,1,128]{2,0,1:T(8,128)(2,1)S(1)}, bf16[384,1,128]{2,0,1:T(8,128)(2,1)}, u32[]{:S(2)}) copy-start(bf16[384,1,128]{2,0,1:T(8,128)(2,1)} %get-tuple-element.11) | copy-start | bytes 294916
  268.8 9.5 %copy-start.8 = (bf16[384,1,128]{0,2,1:T(8,128)(2,1)S(1)}, bf16[384,1,128]{0,2,1:T(8,128)(2,1)}, u32[]{:S(2)}) copy-start(bf16[384,1,128]{0,2,1:T(8,128)(2,1)} %copy.99) | copy-start | bytes 294916
  278.3 11.0 %copy-start.3 = (bf16[1,8,1,128,128]{4,3,2,1,0:T(8,128)(2,1)S(1)}, bf16[1,8,1,128,128]{4,3,2,1,0:T(8,128)(2,1)}, u32[]{:S(2)}) copy-start(bf16[1,8,1,128,128]{4,3,2,1,0:T(8,128)(2,1)} %get-tuple-element.20) | copy-start | bytes 786436
  278.3 11.1 %copy-start.5 = (bf16[384,1,128]{2,0,1:T(8,128)(2,1)S(1)}, bf16[384,1,128]{2,0,1:T(8,128)(2,1)}, u32[]{:S(2)}) copy-start(bf16[384,1,128]{2,0,1:T(8,128)(2,1)} %get-tuple-element.12) | copy-start | bytes 294916
  289.4 17.4 %copy-start.7 = (bf16[384,1,128]{0,2,1:T(8,128)(2,1)S(1)}, bf16[384,1,128]{0,2,1:T(8,128)(2,1)}, u32[]{:S(2)}) copy-start(bf16[384,1,128]{0,2,1:T(8,128)(2,1)} %copy.93) | copy-start | bytes 294916
  306.8 32.7 %copy-start.2 = (bf16[384,1024]{1,0:T(8,128)(2,1)S(1)}, bf16[384,1024]{1,0:T(8,128)(2,1)}, u32[]{:S(2)}) copy-start(bf16[384,1024]{1,0:T(8,128)(2,1)} %copy.115) | copy-start | bytes 2359300
  339.4 1.6 copy-start
